TPU v7x, 32 devices: a whole 2x2x4 slice. The times are simulated.
32 devices in a mesh: row: 8 (over y, x, core), col: 4 (over z).
Axes of the slice: x: 2, y: 2, z: 4, core: 2. Of those that a mesh axis runs over, the one named last changes fastest.
Arguments:
- trials: float32 [2, 512, 1024], P(None, 'col', 'row'), may hold values from -6 to 6
- valence_factor: float32 [16384, 512], P('row'), may hold values from -0.25 to 0.25
- conduction_factor: float32 [16384, 1024], P('col', 'row'), may hold values from -0.046875 to 0.046875
- screened: float32 [16384, 16384], P('row', 'col'), may hold values from -6 to 6
- valence_energy: float32 [512], P('col'), may hold values from -0.6 to -0.1
- conduction_energy: float32 [1024], P('row'), may hold values from 0.1 to 0.6
Outputs:
- applied: float32 [2, 512, 1024], P(None, 'col', 'row')
All inputs are finite; a program needn't handle non-finite values.
Results may differ from a plain program's by a relative error of at most 0.0001.
Values sent between devices are 32-bit elements; how exact they have to be, the bound alone decides.
A program may use at most 256 MiB of HBM per device.

v0:
```python
import jax
import jax.numpy as jnp
from jax import lax
from jax.sharding import PartitionSpec as P


def body(trials, valence_factor, conduction_factor, screened, valence_energy, conduction_energy):
    highest = lax.Precision.HIGHEST
    all_valence = lax.all_gather(trials, "col", axis=1, tiled=True)
    partial_value = jnp.einsum("bvc,nc->bvn", all_valence, conduction_factor, precision=highest)
    points = lax.psum(partial_value, "row")
    expanded = jnp.einsum("mv,bvn->bmn", valence_factor, points, precision=highest)
    weighted = expanded * screened[None]
    folded = jnp.einsum("mv,bmn->bvn", valence_factor, weighted, precision=highest)
    shares = lax.psum_scatter(folded, "row", scatter_dimension=1, tiled=True)
    factor_full = lax.all_gather(conduction_factor, "row", axis=1, tiled=True)
    kernel_rows = jnp.einsum("bvn,nc->bvc", shares, factor_full, precision=highest)
    swapped = lax.all_to_all(kernel_rows, "row", split_axis=2, concat_axis=1, tiled=True)
    kernel_term = lax.psum_scatter(swapped, "col", scatter_dimension=1, tiled=True)
    differences = conduction_energy[None, :] - valence_energy[:, None]
    return differences[None] * trials - kernel_term


def solution(mesh):
    in_specs = (
        P(None, "col", "row"),
        P("row", None),
        P("col", "row"),
        P("row", "col"),
        P("col"),
        P("row"),
    )
    out_specs = P(None, "col", "row")
    return jax.shard_map(body, mesh=mesh, in_specs=in_specs, out_specs=out_specs, check_vma=False)
```

profile of v0, /device:TPU:0, one launch (start us, length us, event | category | flops | bytes accessed | tf_op | source)
XLA Modules:
  0.0 781.5 jit_solution(15031919599068699911)
XLA Ops:
  6.5 0.0 all-reduce.2.cloned.1.call-start
  6.5 17.6 %all_gather.6 = f32[2,512,128]{2,1,0:T(8,128)S(1)} all-gather(f32[2,128,128]{2,1,0:T(8,128)} %param.6), channel_id=1, replica_groups=mesh['row'=8,'col'=4] {'col'}, dimensions={1}, use_global_device_ids=true | all-gather | bytes 655360 | tf_op jit(solution)/shard_map/all_gather | solution.py:9
  24.1 16.8 %fusion.8 = f32[2,512,4096]{2,1,0:T(8,128)} fusion(f32[2,512,128]{2,1,0:T(8,128)S(1)} %all_gather.6, f32[4096,128]{1,0:T(8,128)} %param.8), kind=kOutput, calls=%fused_computation.9 | convolution fusion | flops 6442450944 | bytes 19398656 | tf_op jit(solution)/shard_map/bvc,nc->bvn/dot_general | solution.py:10
  40.9 0.0 all-reduce.2.cloned.1.call-update
  40.9 0.0 all-gather.2.cloned.1.call-start
  41.0 0.7 all-gather.2.cloned.1.call-update
  41.7 0.0 reduce-scatter.3.cloned.1.call-start
  41.7 33.8 %copy.9 = f32[2048,4096]{0,1:T(8,128)} copy(f32[2048,4096]{1,0:T(8,128)} %param.9) | data formatting | bytes 67108864 | tf_op args[3]
  75.5 185.1 %all-reduce.2.cloned.1.call-done = f32[2,512,4096]{2,1,0:T(8,128)} async-done(((f32[2,512,4096]{2,1,0:T(8,128)}), f32[2,512,4096]{2,1,0:T(8,128)}) %all-reduce.2.cloned.1.call-update) | async-done | bytes 16777232 | tf_op jit(solution)/shard_map/psum | solution.py:11
  260.6 217.2 %fusion.6 = f32[2,4096,2048]{2,1,0:T(8,128)} fusion(f32[2,512,4096]{2,1,0:T(8,128)} %all-reduce.2.cloned.1.call-done, f32[2048,512]{1,0:T(8,128)} %param.7), kind=kOutput, calls=%fused_computation.7 | convolution fusion | flops 103079215104 | bytes 88080384 | tf_op jit(solution)/shard_map/mv,bvn->bmn/dot_general | solution.py:12
  477.8 0.0 copy-done
  477.8 125.9 %fusion.4 = f32[2,512,4096]{2,1,0:T(8,128)} fusion(f32[2,4096,2048]{2,1,0:T(8,128)} %fusion.6, f32[2048,4096]{0,1:T(8,128)} %copy.9, f32[2048,512]{1,0:T(8,128)S(1)} %copy-done), kind=kOutput, calls=%fused_computation.5 | convolution fusion | flops 103095992320 | bytes 121634816 | tf_op jit(solution)/shard_map/mv,bmn->bvn/dot_general | solution.py:14
  603.7 0.0 reduce-scatter.3.cloned.1.call-update
  603.8 0.0 copy-start.2
  603.8 0.0 copy-start.3
  603.8 0.0 copy-start.1
  603.8 0.0 reduce-scatter.5.cloned.1.call-start
  603.9 0.0 all-gather.2.cloned.1.call-done
  603.9 116.3 %reduce-scatter.3.cloned.1.call-done = f32[2,64,4096]{2,1,0:T(8,128)} async-done(((f32[2,512,4096]{2,1,0:T(8,128)}), f32[2,64,4096]{2,1,0:T(8,128)}) %reduce-scatter.3.cloned.1.call-update) | async-done | bytes 2097168 | tf_op jit(solution)/shard_map/reduce_scatter | solution.py:15
  720.1 13.6 %fusion.2 = f32[2,64,1024]{2,1,0:T(8,128)S(1)} fusion(f32[2,64,4096]{2,1,0:T(8,128)} %reduce-scatter.3.cloned.1.call-done, f32[4096,1024]{1,0:T(8,128)} %all-gather.2.cloned.1.call-done), kind=kOutput, calls=%fused_computation.3 | convolution fusion | flops 6442450944 | bytes 19398656 | tf_op jit(solution)/shard_map/bvn,nc->bvc/dot_general | solution.py:17
  733.7 0.6 copy.10
  734.3 1.1 reshape.31
  735.4 12.2 %all_to_all.18 = f32[8,1,16384]{2,1,0:T(1,128)S(1)} all-to-all(f32[8,1,16384]{2,1,0:T(1,128)S(1)} %reshape.31), channel_id=1, replica_groups=mesh['row'=8,'col'=4] {'row'}, dimensions={0} | all-to-all | bytes 1048576 | tf_op jit(solution)/shard_map/all_to_all | solution.py:18
  747.6 0.5 broadcast.20
  748.1 1.9 reduce
  750.0 0.8 reshape.32
  750.8 1.2 copy.11
  752.0 0.0 reduce-scatter.5.cloned.1.call-update
  752.0 0.0 copy-done.2
  752.0 0.1 broadcast_subtract_fusion
  752.1 21.0 %reduce-scatter.5.cloned.1.call-done = f32[2,128,128]{2,1,0:T(8,128)} async-done(((f32[2,512,128]{2,1,0:T(8,128)}), f32[2,128,128]{2,1,0:T(8,128)}) %reduce-scatter.5.cloned.1.call-update) | async-done | bytes 131088 | tf_op jit(solution)/shard_map/reduce_scatter | solution.py:19
  773.1 1.6 multiply_subtract_fusion
  (3 shorter events, 0.0 us)
Async XLA Ops:
  6.5 254.1 %all-reduce.2.cloned.1.call-start = ((), (), s32[]{:S(2)}) async-start(), calls=%async_computation.3 | async-start | bytes 33554432 | tf_op jit(solution)/shard_map/psum | solution.py:11
  40.9 563.0 %all-gather.2.cloned.1.call-start = ((), (), s32[]{:S(2)}) async-start(), calls=%async_computation.5 | async-start | bytes 18874368 | tf_op jit(solution)/shard_map/all_gather | solution.py:16
  41.7 678.5 %reduce-scatter.3.cloned.1.call-start = ((), (), s32[]{:S(2)}) async-start(), calls=%async_computation.4 | async-start | bytes 18874368 | tf_op jit(solution)/shard_map/reduce_scatter | solution.py:15
  260.6 217.2 %copy-start = (f32[2048,512]{1,0:T(8,128)S(1)}, f32[2048,512]{1,0:T(8,128)}, u32[]{:S(2)}) copy-start(f32[2048,512]{1,0:T(8,128)} %param.7) | copy-start | bytes 12582916
  603.8 148.2 %copy-start.2 = (f32[128]{0:T(128)S(1)}, f32[128]{0:T(128)}, u32[]{:S(2)}) copy-start(f32[128]{0:T(128)} %param.10) | copy-start | bytes 1540
  603.8 148.2 %copy-start.3 = (f32[128]{0:T(128)S(1)}, f32[128]{0:T(128)}, u32[]{:S(2)}) copy-start(f32[128]{0:T(128)} %param.11) | copy-start | bytes 1540
  603.8 169.3 %copy-start.1 = (f32[2,128,128]{2,1,0:T(8,128)S(1)}, f32[2,128,128]{2,1,0:T(8,128)}, u32[]{:S(2)}) copy-start(f32[2,128,128]{2,1,0:T(8,128)} %param.6) | copy-start | bytes 393220
  603.8 169.3 %reduce-scatter.5.cloned.1.call-start = ((), (), s32[]{:S(2)}) async-start(), calls=%async_computation.6 | async-start | bytes 655360 | tf_op jit(solution)/shard_map/reduce_scatter | solution.py:19
Sparse Core Ops, SparseCore 0:
  41.0 219.5 all-reduce.1
  262.5 93.0 all-gather.1
  603.9 116.1 reduce-scatter.2
  752.1 20.9 reduce-scatter.4
where the time goes:
time: 786 us; the launch traced here: 781 us
  matrix products  373 us (47%)
  waiting for transfers between devices  323 us (41%)
  local copies, waits for them, and re-layouts  38 us (5%)
  blocking collectives  29.8 us (4%)
  between operations  13.4 us (2%)
    dot_general x1, matrix products, body(): jnp.einsum('mv,bvn->bmn', valence_factor, points, precision=highest)  217 us
    psum x1, waiting for transfers between devices, body(): points = lax.psum(partial_value, 'row')  185 us
    dot_general x1, matrix products, body(): jnp.einsum('mv,bmn->bvn', valence_factor, weighted, precision=highest)  126 us
    reduce_scatter x1, waiting for transfers between devices, body(): shares = lax.psum_scatter(folded, 'row', scatter_dimension=1, tiled=True)  116 us
    unnamed x11, local copies, waits for them, and re-layouts  35.7 us
    reduce_scatter x1, waiting for transfers between devices, body(): lax.psum_scatter(swapped, 'col', scatter_dimension=1, tiled=True)  21 us
    all_gather x1, blocking collectives, body(): all_valence = lax.all_gather(trials, 'col', axis=1, tiled=True)  17.6 us
    dot_general x1, matrix products, body(): jnp.einsum('bvc,nc->bvn', all_valence, conduction_factor, precision=highest)  16.8 us
  transfers between devices with their start and end apart: 4, of which 3 were waited for; matrix products, arithmetic and copies ran while one was open for 48% of the time, Pallas kernels for 0%

commit v1 on v0

v1 whole, which is shorter than its diff:
```python
import functools

import jax
import jax.numpy as jnp
from jax import lax
from jax.experimental import pallas as pl
from jax.experimental.pallas import tpu as pltpu
from jax.sharding import PartitionSpec as P


CHUNKS = 4
TILE_M = 1024
TILE_N = 512
ROWS = 1024


def split(x):
    high = lax.reduce_precision(x, 8, 7)
    return high.astype(jnp.bfloat16), (x - high).astype(jnp.bfloat16)


def split_in_kernel(x):
    high = x.astype(jnp.bfloat16)
    return high, (x - high.astype(jnp.float32)).astype(jnp.bfloat16)


def dot3(a, b, depth_of_b=0):
    left = jnp.concatenate([a[0], a[0], a[1]], axis=1)
    right = jnp.concatenate([b[0], b[1], b[0]], axis=depth_of_b)
    dims = (((1,), (depth_of_b,)), ((), ()))
    return lax.dot_general(left, right, dims, preferred_element_type=jnp.float32)


def local_kernel(limits, first, vh, vl, wh, wl, trials, screened, *refs):
    factors, refs = refs[:len(limits)], refs[len(limits):]
    if not first:
        before, refs = refs[0], refs[1:]
    out, th, tl, ch, cl, ph, pw, folded = refs
    j, i = pl.program_id(0), pl.program_id(1)
    steps = pl.num_programs(1)
    pieces, width = trials.shape[0], trials.shape[2]
    tile_m = screened.shape[0]
    rows = min(ROWS, tile_m)

    def whole(ref):
        return jnp.concatenate([ref[p] for p in range(pieces)], axis=1) if pieces > 1 else ref[0]

    @pl.when((j == 0) & (i == 0))
    def _():
        th[...], tl[...] = split_in_kernel(whole(trials))
        out[...] = jnp.zeros_like(out) if first else before[...]

    for (low, high), factor in zip(limits, factors):

        @pl.when((i == 0) & (j >= low) & (j < high))
        def _():
            ch[...], cl[...] = split_in_kernel(whole(factor))

    @pl.when(i == 0)
    def _():
        points = dot3((th[...], tl[...]), (ch[...], cl[...]), 1)
        ph[...], pw[...] = split_in_kernel(points)

    total = None
    for u in range(tile_m // rows):
        at = pl.ds(pl.multiple_of(i * tile_m + u * rows, rows), rows)
        expanded = dot3((vh[at, :], vl[at, :]), (ph[...], pw[...]))
        weighted = expanded * screened[u * rows:(u + 1) * rows, :]
        term = dot3((wh[:, at], wl[:, at]), split_in_kernel(weighted))
        total = term if total is None else total + term
    folded[...] = jnp.where(i == 0, total, folded[...] + total) if steps > 1 else total

    @pl.when(i == steps - 1)
    def _():
        term = dot3(split_in_kernel(folded[...]), (ch[...], cl[...]))
        blocks, part = out.shape[1], out.shape[2]
        for p in range(pieces):
            for q in range(blocks):
                out[p, q] += term[q * part:(q + 1) * part, p * width:(p + 1) * width]


def local_term(start, valence, valence_t, trials, screened, factors, before, blocks):
    pieces, depth, width = trials.shape
    rows = valence[0].shape[0]
    count = factors[0].shape[1]
    tile_m, tile_n = min(TILE_M, rows), min(TILE_N, count)
    tiles = count // tile_n
    limits = tuple((k * tiles, (k + 1) * tiles) for k in range(len(factors)))
    offset = start // tile_n
    first = before is None
    out_shape = (pieces, blocks, depth // blocks, width)
    keep = lambda shape: pl.BlockSpec(shape, lambda j, i: (0,) * len(shape), pipeline_mode=pl.Buffered(1))
    operands = [*valence, *valence_t, trials, screened, *factors]
    in_specs = [keep(x.shape) for x in operands[:5]]
    in_specs.append(pl.BlockSpec((tile_m, tile_n), lambda j, i: (i, j + offset)))
    for low, high in limits:
        in_specs.append(pl.BlockSpec((pieces, tile_n, width), functools.partial(
            lambda low, high, j, i: (0, jnp.clip(j, low, high - 1) - low, 0), low, high)))
    if not first:
        operands.append(before)
        in_specs.append(keep(out_shape))
    points = count * len(factors)
    conduction = pieces * width
    half = lambda *shape: pltpu.VMEM(shape, jnp.bfloat16)
    return pl.pallas_call(
        functools.partial(local_kernel, limits, first),
        out_shape=jax.ShapeDtypeStruct(out_shape, jnp.float32),
        grid=(tiles * len(factors), rows // tile_m),
        in_specs=in_specs,
        out_specs=keep(out_shape),
        scratch_shapes=[
            half(depth, conduction), half(depth, conduction),
            half(tile_n, conduction), half(tile_n, conduction),
            half(depth, tile_n), half(depth, tile_n),
            pltpu.VMEM((depth, tile_n), jnp.float32),
        ],
        compiler_params=pltpu.CompilerParams(vmem_limit_bytes=60 * 1024 * 1024),
        cost_estimate=pl.CostEstimate(
            flops=12 * depth * points * (rows + conduction), bytes_accessed=4 * rows * points, transcendentals=0),
        name="local_term",
    )(*operands)


def body(trials, valence_factor, conduction_factor, screened, valence_energy, conduction_energy):
    row, col = lax.axis_size("row"), lax.axis_size("col")
    batch, part, width = trials.shape
    count = conduction_factor.shape[0] // CHUNKS
    aligned = width % 128 == 0

    def gather(x):
        return lax.all_gather(x, "row") if aligned else lax.all_gather(x, "row", axis=1, tiled=True)[None]

    factors = [gather(conduction_factor[k * count:(k + 1) * count]) for k in range(CHUNKS)]
    every = lax.all_gather(trials, "col", axis=1, tiled=True)
    vectors = [gather(every[b]) for b in range(batch)]
    valence, valence_t = split(valence_factor), split(valence_factor.T)
    totals = [None] * batch

    def add(b, low, high):
        totals[b] = local_term(
            low * count, valence, valence_t, vectors[b], screened, factors[low:high], totals[b], col)

    def owned(b):
        total = totals[b]
        if not aligned:
            total = total[0].reshape(col, part, row, width).transpose(2, 0, 1, 3)
        return lax.psum_scatter(total, "row")

    half = CHUNKS // 2
    for b in range(batch):
        if b == 0:
            for k in range(half):
                add(b, k, k + 1)
        else:
            add(b, 0, half)
    totals = list(lax.optimization_barrier(tuple(totals)))
    terms = []
    for b in range(batch):
        if b == 0:
            for k in range(half, CHUNKS):
                add(b, k, k + 1)
        else:
            add(b, half, CHUNKS)
        terms.append(owned(b))
    swapped = lax.all_to_all(jnp.stack(terms, axis=1), "col", split_axis=0, concat_axis=0, tiled=True)
    kernel_term = swapped.sum(axis=0)
    differences = conduction_energy[None, :] - valence_energy[:, None]
    return differences[None] * trials - kernel_term


def solution(mesh):
    in_specs = (
        P(None, "col", "row"),
        P("row", None),
        P("col", "row"),
        P("row", "col"),
        P("col"),
        P("row"),
    )
    out_specs = P(None, "col", "row")
    return jax.shard_map(body, mesh=mesh, in_specs=in_specs, out_specs=out_specs, check_vma=False)
```

time: 786 us -> 394 us (0.50)
  matrix products: 373 us -> 0 us
  Pallas kernels: 0 us -> 221 us
  waiting for transfers between devices: 323 us -> 117 us
  local copies, waits for them, and re-layouts: 38 us -> 10.1 us
  blocking collectives: 29.8 us -> 17.6 us
    dot_general x4 -> x0, matrix products: 373 us -> none  [the longest x1 217 us: body(): jnp.einsum('mv,bvn->bmn', valence_factor, points, precision=highest)]
    pallas_call x0 -> x6, Pallas kernels: none -> 221 us  [local_term(): pl.pallas_call(functools.partial(local_kernel, limits, first), out_shape=...]
    psum x1 -> x0, waiting for transfers between devices: 185 us -> none  [body(): points = lax.psum(partial_value, 'row')]
    reduce_scatter x2, waiting for transfers between devices: 137 us -> 41.2 us  [owned(): return lax.psum_scatter(total, 'row')]
    all_gather x1 -> x6, waiting for transfers between devices: 0.02 us -> 59.3 us  [gather(): lax.all_gather(x, 'row')]
    unnamed x11 -> x9, local copies, waits for them, and re-layouts: 35.7 us -> 5.52 us
    all_to_all x0 -> x1, waiting for transfers between devices: none -> 14.3 us  [body(): lax.all_to_all(jnp.stack(terms, axis=1), 'col', split_axis=0, concat_axis...]
    all_to_all x1 -> x0, blocking collectives: 12.2 us -> none  [body(): lax.all_to_all(kernel_rows, 'row', split_axis=2, concat_axis=1, tiled=True)]
  transfers between devices with their start and end apart: 4 -> 9, of which waited for: 3 -> 6; matrix products, arithmetic and copies ran while one was open for 48% -> 4% of each run, Pallas kernels for 0% -> 49%
where the time goes in v1:
time: 394 us
  Pallas kernels  221 us (56%)
  waiting for transfers between devices  117 us (30%)
  blocking collectives  17.6 us (4%)
  between operations  13.6 us (3%)
  local copies, waits for them, and re-layouts  10.1 us (3%)
  other arithmetic  9.77 us (2%)
  starting transfers between devices  4.88 us (1%)
    pallas_call x6, Pallas kernels, local_term(): pl.pallas_call(functools.partial(local_kernel, limits, first), out_shape=...  221 us
    all_gather x6, waiting for transfers between devices, gather(): lax.all_gather(x, 'row')  59.3 us
    reduce_scatter x2, waiting for transfers between devices, owned(): return lax.psum_scatter(total, 'row')  41.2 us
    all_gather x1, blocking collectives, body(): every = lax.all_gather(trials, 'col', axis=1, tiled=True)  17.6 us
    all_to_all x1, waiting for transfers between devices, body(): lax.all_to_all(jnp.stack(terms, axis=1), 'col', split_axis=0, concat_axis...  14.3 us
    convert_element_type x2, other arithmetic, split(): return (high.astype(jnp.bfloat16), (x - high).astype(jnp.bfloat16))  7.93 us
  transfers between devices with their start and end apart: 9, of which 6 were waited for; matrix products, arithmetic and copies ran while one was open for 4% of the time, Pallas kernels for 49%

profile of v1, /device:TPU:0, one launch (start us, length us, event | category | flops | bytes accessed | tf_op | source)
XLA Modules:
  0.0 393.9 jit_solution(12842054423644248568)
XLA Ops:
  6.5 17.6 %all_gather.33 = f32[2,512,128]{2,1,0:T(8,128)S(1)} all-gather(f32[2,128,128]{2,1,0:T(8,128)} %param.6), channel_id=1, replica_groups=mesh['row'=8,'col'=4] {'col'}, dimensions={1}, use_global_device_ids=true | all-gather | bytes 655360 | tf_op jit(solution)/shard_map/all_gather | solution.py:134
  24.1 0.9 fusion.3
  25.0 0.0 all-gather.21.cloned.1.call-start
  25.0 2.9 fusion.2
  28.0 0.0 all-gather.19.cloned.1.call-start
  28.0 0.7 all-gather.19.cloned.1.call-update
  28.7 0.0 all-gather.13.cloned.1.call-start
  28.7 0.5 all-gather.13.cloned.1.call-update
  29.3 0.5 all-gather.17.cloned.1.call-update
  29.9 0.5 all-gather.15.cloned.1.call-update
  30.4 0.0 reduce-scatter.3.cloned.1.call-start
  30.5 5.5 %copy.8 = f32[2048,512]{0,1:T(8,128)} copy(f32[2048,512]{1,0:T(8,128)} %param.7) | data formatting | bytes 8388608 | tf_op args[1]
  36.0 5.1 %fusion = (bf16[2048,512]{1,0:T(8,128)(2,1)}, bf16[2048,512]{1,0:T(8,128)(2,1)}) fusion(f32[2048,512]{1,0:T(8,128)} %param.7), kind=kLoop, calls=%fused_computation.4 | loop fusion | flops 4194304 | bytes 8388608 | tf_op jit(solution)/shard_map/convert_element_type | solution.py:19
  41.0 2.9 fusion.1
  43.9 10.8 %all-gather.11.cloned.1.call-done.trials = f32[8,512,128]{2,1,0:T(8,128)} async-done(((f32[1,512,128]{2,1,0:T(8,128)}), f32[8,512,128]{2,1,0:T(8,128)}) %all-gather.11.cloned.1.call-update) | async-done | bytes 2097168 | tf_op jit(solution)/shard_map/all_gather | solution.py:131
  54.7 38.5 %all-gather.21.cloned.1.call-done = f32[8192,128]{1,0:T(8,128)} async-done(((f32[1024,128]{1,0:T(8,128)}), f32[8192,128]{1,0:T(8,128)}) %all-gather.21.cloned.1.call-update) | async-done | bytes 4194320 | tf_op jit(solution)/shard_map/all_gather | solution.py:131
  93.2 28.7 %local_term.6.refs_1_ = f32[8,4,128,128]{3,2,1,0:T(8,128)} custom-call(bf16[2048,512]{1,0:T(8,128)(2,1)} %get-tuple-element.12.vh, bf16[2048,512]{1,0:T(8,128)(2,1)} %get-tuple-element.11.vl, bf16[512,2048]{1,0:T(8,128)(2,1)} %get-tuple-element.10.wh, bf16[512,2048]{1,0:T(8,128)(2,1)} %get-tuple-element.9.wl, ...), custom_call_target="tpu_custom_call" | custom-call | flops 19327352832 | bytes 8388608 | tf_op jit(solution)/shard_map/local_term/pallas_call | solution.py:105
  121.9 9.8 %all-gather.19.cloned.1.call-done = f32[8192,128]{1,0:T(8,128)} async-done(((f32[1024,128]{1,0:T(8,128)}), f32[8192,128]{1,0:T(8,128)}) %all-gather.19.cloned.1.call-update) | async-done | bytes 4194320 | tf_op jit(solution)/shard_map/all_gather | solution.py:131
  131.7 29.3 %local_term.7.refs_1_ = f32[8,4,128,128]{3,2,1,0:T(8,128)} custom-call(bf16[2048,512]{1,0:T(8,128)(2,1)} %get-tuple-element.12.vh, bf16[2048,512]{1,0:T(8,128)(2,1)} %get-tuple-element.11.vl, bf16[512,2048]{1,0:T(8,128)(2,1)} %get-tuple-element.10.wh, bf16[512,2048]{1,0:T(8,128)(2,1)} %get-tuple-element.9.wl, ...), custom_call_target="tpu_custom_call" | custom-call | flops 19327352832 | bytes 8388608 | tf_op jit(solution)/shard_map/local_term/pallas_call | solution.py:105
  161.0 0.2 all-gather.13.cloned.1.call-done.trials
  161.3 51.3 %local_term.8.refs_2_ = f32[8,4,128,128]{3,2,1,0:T(8,128)} custom-call(bf16[2048,512]{1,0:T(8,128)(2,1)} %get-tuple-element.12.vh, bf16[2048,512]{1,0:T(8,128)(2,1)} %get-tuple-element.11.vl, bf16[512,2048]{1,0:T(8,128)(2,1)} %get-tuple-element.10.wh, bf16[512,2048]{1,0:T(8,128)(2,1)} %get-tuple-element.9.wl, ...), custom_call_target="tpu_custom_call" | custom-call | flops 38654705664 | bytes 16777216 | tf_op jit(solution)/shard_map/local_term/pallas_call | solution.py:105
  212.6 29.6 %local_term.9.refs_1_ = f32[8,4,128,128]{3,2,1,0:T(8,128)} custom-call(bf16[2048,512]{1,0:T(8,128)(2,1)} %get-tuple-element.12.vh, bf16[2048,512]{1,0:T(8,128)(2,1)} %get-tuple-element.11.vl, bf16[512,2048]{1,0:T(8,128)(2,1)} %get-tuple-element.10.wh, bf16[512,2048]{1,0:T(8,128)(2,1)} %get-tuple-element.9.wl, ...), custom_call_target="tpu_custom_call" | custom-call | flops 19327352832 | bytes 8388608 | tf_op jit(solution)/shard_map/local_term/pallas_call | solution.py:105
  242.2 29.4 %local_term.10 = f32[8,4,128,128]{3,2,1,0:T(8,128)} custom-call(bf16[2048,512]{1,0:T(8,128)(2,1)} %get-tuple-element.12.vh, bf16[2048,512]{1,0:T(8,128)(2,1)} %get-tuple-element.11.vl, bf16[512,2048]{1,0:T(8,128)(2,1)} %get-tuple-element.10.wh, bf16[512,2048]{1,0:T(8,128)(2,1)} %get-tuple-element.9.wl, f32[8,512,128]{2,1,0:T(8,128)} %all-gather.11.cloned.1.call-done.trials, ...), custom_call_target="tpu_custom_call" | custom-call | flops 19327352832 | bytes 8388608 | tf_op jit(solution)/shard_map/local_term/pallas_call | solution.py:105
  271.7 0.0 reduce-scatter.5.cloned.1.call-start
  271.7 52.5 %local_term.11 = f32[8,4,128,128]{3,2,1,0:T(8,128)} custom-call(bf16[2048,512]{1,0:T(8,128)(2,1)} %get-tuple-element.12.vh, bf16[2048,512]{1,0:T(8,128)(2,1)} %get-tuple-element.11.vl, bf16[512,2048]{1,0:T(8,128)(2,1)} %get-tuple-element.10.wh, bf16[512,2048]{1,0:T(8,128)(2,1)} %get-tuple-element.9.wl, f32[8,512,128]{2,1,0:T(8,128)} %all-gather.13.cloned.1.call-done.trials, ...), custom_call_target="tpu_custom_call" | custom-call | flops 38654705664 | bytes 16777216 | tf_op jit(solution)/shard_map/local_term/pallas_call | solution.py:105
  324.3 41.2 %reduce-scatter.5.cloned.1.call-done = f32[1,4,128,128]{3,2,1,0:T(8,128)} async-done(((f32[8,4,128,128]{3,2,1,0:T(8,128)}), f32[1,4,128,128]{3,2,1,0:T(8,128)}) %reduce-scatter.5.cloned.1.call-update) | async-done | bytes 262160 | tf_op jit(solution)/shard_map/reduce_scatter | solution.py:147
  365.5 1.1 pad_maximum_fusion
  366.6 0.8 copy.9
  367.4 4.6 %all-to-all-start = ((f32[4,2,128,128]{3,2,1,0:T(8,128)}), f32[4,2,128,128]{3,2,1,0:T(8,128)S(1)}, u32[]{:S(2)}, u32[]{:S(2)}) async-start(f32[4,2,128,128]{3,2,1,0:T(8,128)} %copy.9), calls=%async_computation.2 | async-start | bytes 1048576 | tf_op jit(solution)/shard_map/all_to_all | solution.py:165
  372.0 0.1 broadcast_subtract_fusion
  372.1 14.3 %all-to-all-done = f32[4,2,128,128]{3,2,1,0:T(8,128)S(1)} async-done(((f32[4,2,128,128]{3,2,1,0:T(8,128)}), f32[4,2,128,128]{3,2,1,0:T(8,128)S(1)}, u32[]{:S(2)}, u32[]{:S(2)}) %all-to-all-start) | async-done | bytes 524320 | tf_op jit(solution)/shard_map/all_to_all | solution.py:165
  386.4 0.7 multiply_subtract_fusion
  (19 shorter events, 0.2 us)
Async XLA Ops:
  6.5 48.2 %all-gather.11.cloned.1.call-start = ((), (), s32[]{:S(2)}) async-start(), calls=%async_computation.3 | async-start | bytes 2359296 | tf_op jit(solution)/shard_map/all_gather | solution.py:131
  25.0 68.2 %all-gather.21.cloned.1.call-start = ((), (), s32[]{:S(2)}) async-start(), calls=%async_computation.10 | async-start | bytes 4718592 | tf_op jit(solution)/shard_map/all_gather | solution.py:131
  28.0 103.7 %all-gather.19.cloned.1.call-start = ((), (), s32[]{:S(2)}) async-start(), calls=%async_computation.9 | async-start | bytes 4718592 | tf_op jit(solution)/shard_map/all_gather | solution.py:131
  28.7 132.6 %all-gather.13.cloned.1.call-start = ((), (), s32[]{:S(2)}) async-start(), calls=%async_computation.4 | async-start | bytes 2359296 | tf_op jit(solution)/shard_map/all_gather | solution.py:131
  29.3 183.3 %all-gather.17.cloned.1.call-start = ((), (), s32[]{:S(2)}) async-start(), calls=%async_computation.8 | async-start | bytes 4718592 | tf_op jit(solution)/shard_map/all_gather | solution.py:131
  29.9 212.3 %all-gather.15.cloned.1.call-start = ((), (), s32[]{:S(2)}) async-start(), calls=%async_computation.7 | async-start | bytes 4718592 | tf_op jit(solution)/shard_map/all_gather | solution.py:131
  30.4 293.9 %reduce-scatter.3.cloned.1.call-start = ((), (), s32[]{:S(2)}) async-start(), calls=%async_computation.5 | async-start | bytes 2359296 | tf_op jit(solution)/shard_map/reduce_scatter | solution.py:147
  36.0 5.1 %copy-start = (f32[2048,512]{0,1:T(8,128)S(1)}, f32[2048,512]{0,1:T(8,128)}, u32[]{:S(2)}) copy-start(f32[2048,512]{0,1:T(8,128)} %copy.8) | copy-start | bytes 12582916
  271.7 93.8 %reduce-scatter.5.cloned.1.call-start = ((), (), s32[]{:S(2)}) async-start(), calls=%async_computation.6 | async-start | bytes 2359296 | tf_op jit(solution)/shard_map/reduce_scatter | solution.py:147
  324.2 47.8 %copy-start.2 = (f32[128]{0:T(128)S(1)}, f32[128]{0:T(128)}, u32[]{:S(2)}) copy-start(f32[128]{0:T(128)} %param.10) | copy-start | bytes 1540
  324.2 47.7 %copy-start.3 = (f32[128]{0:T(128)S(1)}, f32[128]{0:T(128)}, u32[]{:S(2)}) copy-start(f32[128]{0:T(128)} %param.11) | copy-start | bytes 1540
  324.3 62.1 %copy-start.1 = (f32[2,128,128]{2,1,0:T(8,128)S(1)}, f32[2,128,128]{2,1,0:T(8,128)}, u32[]{:S(2)}) copy-start(f32[2,128,128]{2,1,0:T(8,128)} %param.6) | copy-start | bytes 393220
  367.4 18.9 %all-to-all-start = ((f32[4,2,128,128]{3,2,1,0:T(8,128)}), f32[4,2,128,128]{3,2,1,0:T(8,128)S(1)}, u32[]{:S(2)}, u32[]{:S(2)}) async-start(f32[4,2,128,128]{3,2,1,0:T(8,128)} %copy.9), calls=%async_computation.2 | async-start | bytes 1048576 | tf_op jit(solution)/shard_map/all_to_all | solution.py:165
Sparse Core Ops, SparseCore 0:
  25.1 29.5 all-gather.10
  56.6 36.5 all-gather.20
  95.1 36.5 all-gather.18
  133.4 27.7 all-gather.12
  163.0 36.5 all-gather.16
  201.4 36.5 all-gather.14
  271.8 41.0 reduce-scatter.2
  324.4 41.0 reduce-scatter.4

commit v2 on v1

--- a/solution.py
+++ b/solution.py
@@ -132,7 +132,11 @@
 
     factors = [gather(conduction_factor[k * count:(k + 1) * count]) for k in range(CHUNKS)]
     every = lax.all_gather(trials, "col", axis=1, tiled=True)
-    vectors = [gather(every[b]) for b in range(batch)]
+    copies = jnp.broadcast_to(every[0], (row,) + every[0].shape)
+    first = lax.all_to_all(copies, "row", split_axis=0, concat_axis=0, tiled=True)
+    if not aligned:
+        first = first.transpose(1, 0, 2).reshape(1, part * col, row * width)
+    vectors = [first] + [gather(every[b]) for b in range(1, batch)]
     valence, valence_t = split(valence_factor), split(valence_factor.T)
     totals = [None] * batch
 
@@ -144,7 +148,9 @@
         total = totals[b]
         if not aligned:
             total = total[0].reshape(col, part, row, width).transpose(2, 0, 1, 3)
-        return lax.psum_scatter(total, "row")
+        if b < batch - 1:
+            return lax.psum_scatter(total, "row")
+        return lax.all_to_all(total, "row", split_axis=0, concat_axis=0, tiled=True).sum(axis=0)
 
     half = CHUNKS // 2
     for b in range(batch):

time: 394 us -> 366 us (0.929); the launches traced: 394 us -> 360 us
  waiting for transfers between devices: 117 us -> 46.2 us
  blocking collectives: 17.6 us -> 47.4 us
    all_gather x6 -> x5, waiting for transfers between devices: 59.3 us -> 8.13 us  [gather(): lax.all_gather(x, 'row')]
    reduce_scatter x2 -> x1, waiting for transfers between devices: 41.2 us -> 0.02 us  [owned(): return lax.psum_scatter(total, 'row')]
    all_to_all x0 -> x1, blocking collectives: none -> 30.1 us  [owned(): lax.all_to_all(total, 'row', split_axis=0, concat_axis=0, tiled=True)]
    all_to_all x0 -> x1, waiting for transfers between devices: none -> 22.4 us  [body(): lax.all_to_all(copies, 'row', split_axis=0, concat_axis=0, tiled=True)]
  transfers between devices with their start and end apart: 9 -> 8, of which waited for: 6 -> 4; matrix products, arithmetic and copies ran while one was open for 4% -> 4% of each run, Pallas kernels for 49% -> 53%
where the time goes in v2:
time: 366 us; the launch traced here: 360 us
  Pallas kernels  221 us (60%)
  blocking collectives  47.4 us (13%)
  waiting for transfers between devices  46.2 us (13%)
  between operations  13.7 us (4%)
  local copies, waits for them, and re-layouts  12.7 us (3%)
  other arithmetic  9.97 us (3%)
  starting transfers between devices  8.53 us (2%)
    pallas_call x6, Pallas kernels, local_term(): pl.pallas_call(functools.partial(local_kernel, limits, first), out_shape=...  221 us
    all_to_all x1, blocking collectives, owned(): lax.all_to_all(total, 'row', split_axis=0, concat_axis=0, tiled=True)  30.1 us
    all_to_all x1, waiting for transfers between devices, body(): lax.all_to_all(copies, 'row', split_axis=0, concat_axis=0, tiled=True)  22.4 us
    all_gather x1, blocking collectives, body(): every = lax.all_gather(trials, 'col', axis=1, tiled=True)  17.4 us
    all_to_all x1, waiting for transfers between devices, body(): lax.all_to_all(jnp.stack(terms, axis=1), 'col', split_axis=0, concat_axis...  13.8 us
    all_gather x5, waiting for transfers between devices, gather(): lax.all_gather(x, 'row')  8.13 us
    convert_element_type x2, other arithmetic, split(): return (high.astype(jnp.bfloat16), (x - high).astype(jnp.bfloat16))  8.05 us
  transfers between devices with their start and end apart: 8, of which 4 were waited for; matrix products, arithmetic and copies ran while one was open for 4% of the time, Pallas kernels for 53%

profile of v2, /device:TPU:0, one launch (start us, length us, event | category | flops | bytes accessed | tf_op | source)
XLA Modules:
  0.0 359.9 jit_solution(9002867607520868954)
XLA Ops:
  6.5 2.9 fusion.2
  9.5 0.0 all-gather.16.cloned.1.call-start
  9.5 0.7 all-gather.16.cloned.1.call-update
  10.2 0.0 all-gather.10.cloned.1.call-start
  10.3 17.4 %all_gather.30 = f32[2,512,128]{2,1,0:T(8,128)S(1)} all-gather(f32[2,128,128]{2,1,0:T(8,128)S(1)} %copy-done.2), channel_id=1, replica_groups=mesh['row'=8,'col'=4] {'col'}, dimensions={1}, use_global_device_ids=true | all-gather | bytes 655360 | tf_op jit(solution)/shard_map/all_gather | solution.py:134
  27.7 0.7 slice_bitcast_fusion
  28.4 0.0 all-gather.14.cloned.1.call-start
  28.5 0.5 all-gather.14.cloned.1.call-update
  29.0 1.5 broadcast_in_dim.2
  30.5 3.7 %all-to-all-start = ((f32[8,512,128]{2,1,0:T(8,128)}), f32[8,512,128]{2,1,0:T(8,128)S(1)}, u32[]{:S(2)}, u32[]{:S(2)}) async-start(f32[8,512,128]{2,1,0:T(8,128)} %broadcast_in_dim.2), calls=%async_computation | async-start | bytes 4194304 | tf_op jit(solution)/shard_map/all_to_all | solution.py:136
  34.3 0.5 all-gather.12.cloned.1.call-update
  34.8 5.4 %copy.8 = f32[2048,512]{0,1:T(8,128)} copy(f32[2048,512]{1,0:T(8,128)} %param.7) | data formatting | bytes 8388608 | tf_op args[1]
  40.2 5.2 %fusion = (bf16[2048,512]{1,0:T(8,128)(2,1)}, bf16[2048,512]{1,0:T(8,128)(2,1)}) fusion(f32[2048,512]{1,0:T(8,128)} %param.7), kind=kLoop, calls=%fused_computation.4 | loop fusion | flops 4194304 | bytes 8388608 | tf_op jit(solution)/shard_map/convert_element_type | solution.py:19
  45.4 2.9 fusion.1
  48.3 22.4 %all-to-all-done.trials = f32[8,512,128]{2,1,0:T(8,128)S(1)} async-done(((f32[8,512,128]{2,1,0:T(8,128)}), f32[8,512,128]{2,1,0:T(8,128)S(1)}, u32[]{:S(2)}, u32[]{:S(2)}) %all-to-all-start) | async-done | bytes 2097184 | tf_op jit(solution)/shard_map/all_to_all | solution.py:136
  70.7 1.3 copy-done.1
  72.0 28.7 %local_term.6.refs_1_ = f32[8,4,128,128]{3,2,1,0:T(8,128)} custom-call(bf16[2048,512]{1,0:T(8,128)(2,1)} %get-tuple-element.12.vh, bf16[2048,512]{1,0:T(8,128)(2,1)} %get-tuple-element.11.vl, bf16[512,2048]{1,0:T(8,128)(2,1)} %get-tuple-element.10.wh, bf16[512,2048]{1,0:T(8,128)(2,1)} %get-tuple-element.9.wl, f32[8,512,128]{2,1,0:T(8,128)} %copy-done.1, ...), custom_call_target="tpu_custom_call" | custom-call | flops 19327352832 | bytes 8388608 | tf_op jit(solution)/shard_map/local_term/pallas_call | solution.py:105
  100.7 8.0 %all-gather.16.cloned.1.call-done = f32[8192,128]{1,0:T(8,128)} async-done(((f32[1024,128]{1,0:T(8,128)}), f32[8192,128]{1,0:T(8,128)}) %all-gather.16.cloned.1.call-update) | async-done | bytes 4194320 | tf_op jit(solution)/shard_map/all_gather | solution.py:131
  108.7 29.6 %local_term.7.refs_1_ = f32[8,4,128,128]{3,2,1,0:T(8,128)} custom-call(bf16[2048,512]{1,0:T(8,128)(2,1)} %get-tuple-element.12.vh, bf16[2048,512]{1,0:T(8,128)(2,1)} %get-tuple-element.11.vl, bf16[512,2048]{1,0:T(8,128)(2,1)} %get-tuple-element.10.wh, bf16[512,2048]{1,0:T(8,128)(2,1)} %get-tuple-element.9.wl, f32[8,512,128]{2,1,0:T(8,128)} %copy-done.1, ...), custom_call_target="tpu_custom_call" | custom-call | flops 19327352832 | bytes 8388608 | tf_op jit(solution)/shard_map/local_term/pallas_call | solution.py:105
  138.3 0.1 all-gather.10.cloned.1.call-done.trials
  138.4 51.4 %local_term.8.refs_2_ = f32[8,4,128,128]{3,2,1,0:T(8,128)} custom-call(bf16[2048,512]{1,0:T(8,128)(2,1)} %get-tuple-element.12.vh, bf16[2048,512]{1,0:T(8,128)(2,1)} %get-tuple-element.11.vl, bf16[512,2048]{1,0:T(8,128)(2,1)} %get-tuple-element.10.wh, bf16[512,2048]{1,0:T(8,128)(2,1)} %get-tuple-element.9.wl, ...), custom_call_target="tpu_custom_call" | custom-call | flops 38654705664 | bytes 16777216 | tf_op jit(solution)/shard_map/local_term/pallas_call | solution.py:105
  189.8 29.9 %local_term.9.refs_1_ = f32[8,4,128,128]{3,2,1,0:T(8,128)} custom-call(bf16[2048,512]{1,0:T(8,128)(2,1)} %get-tuple-element.12.vh, bf16[2048,512]{1,0:T(8,128)(2,1)} %get-tuple-element.11.vl, bf16[512,2048]{1,0:T(8,128)(2,1)} %get-tuple-element.10.wh, bf16[512,2048]{1,0:T(8,128)(2,1)} %get-tuple-element.9.wl, f32[8,512,128]{2,1,0:T(8,128)} %copy-done.1, ...), custom_call_target="tpu_custom_call" | custom-call | flops 19327352832 | bytes 8388608 | tf_op jit(solution)/shard_map/local_term/pallas_call | solution.py:105
  219.7 29.4 %local_term.10 = f32[8,4,128,128]{3,2,1,0:T(8,128)} custom-call(bf16[2048,512]{1,0:T(8,128)(2,1)} %get-tuple-element.12.vh, bf16[2048,512]{1,0:T(8,128)(2,1)} %get-tuple-element.11.vl, bf16[512,2048]{1,0:T(8,128)(2,1)} %get-tuple-element.10.wh, bf16[512,2048]{1,0:T(8,128)(2,1)} %get-tuple-element.9.wl, f32[8,512,128]{2,1,0:T(8,128)} %copy-done.1, ...), custom_call_target="tpu_custom_call" | custom-call | flops 19327352832 | bytes 8388608 | tf_op jit(solution)/shard_map/local_term/pallas_call | solution.py:105
  249.1 52.4 %local_term.11 = f32[8,4,128,128]{3,2,1,0:T(8,128)} custom-call(bf16[2048,512]{1,0:T(8,128)(2,1)} %get-tuple-element.12.vh, bf16[2048,512]{1,0:T(8,128)(2,1)} %get-tuple-element.11.vl, bf16[512,2048]{1,0:T(8,128)(2,1)} %get-tuple-element.10.wh, bf16[512,2048]{1,0:T(8,128)(2,1)} %get-tuple-element.9.wl, f32[8,512,128]{2,1,0:T(8,128)} %all-gather.10.cloned.1.call-done.trials, ...), custom_call_target="tpu_custom_call" | custom-call | flops 38654705664 | bytes 16777216 | tf_op jit(solution)/shard_map/local_term/pallas_call | solution.py:105
  301.5 30.1 %all_to_all.15 = f32[8,4,128,128]{3,2,1,0:T(8,128)S(1)} all-to-all(f32[8,4,128,128]{3,2,1,0:T(8,128)} %local_term.11), channel_id=1, replica_groups=mesh['row'=8,'col'=4] {'row'}, dimensions={0} | all-to-all | bytes 4194304 | tf_op jit(solution)/shard_map/all_to_all | solution.py:153
  331.6 0.1 reduce_sum.18
  331.8 1.0 pad_maximum_fusion
  332.8 0.8 copy.9
  333.6 4.6 %all-to-all-start.2 = ((f32[4,2,128,128]{3,2,1,0:T(8,128)}), f32[4,2,128,128]{3,2,1,0:T(8,128)S(1)}, u32[]{:S(2)}, u32[]{:S(2)}) async-start(f32[4,2,128,128]{3,2,1,0:T(8,128)} %copy.9), calls=%async_computation.3 | async-start | bytes 1048576 | tf_op jit(solution)/shard_map/all_to_all | solution.py:171
  338.2 0.1 broadcast_subtract_fusion
  338.3 13.8 %all-to-all-done.2 = f32[4,2,128,128]{3,2,1,0:T(8,128)S(1)} async-done(((f32[4,2,128,128]{3,2,1,0:T(8,128)}), f32[4,2,128,128]{3,2,1,0:T(8,128)S(1)}, u32[]{:S(2)}, u32[]{:S(2)}) %all-to-all-start.2) | async-done | bytes 524320 | tf_op jit(solution)/shard_map/all_to_all | solution.py:171
  352.2 0.7 multiply_subtract_fusion
  (22 shorter events, 0.2 us)
Async XLA Ops:
  6.5 3.8 %copy-start.2 = (f32[2,128,128]{2,1,0:T(8,128)S(1)}, f32[2,128,128]{2,1,0:T(8,128)}, u32[]{:S(2)}) copy-start(f32[2,128,128]{2,1,0:T(8,128)} %param.6) | copy-start | bytes 393220
  6.5 64.1 %all-gather.18.cloned.1.call-start = ((), (), s32[]{:S(2)}) async-start(), calls=%async_computation.9 | async-start | bytes 4718592 | tf_op jit(solution)/shard_map/all_gather | solution.py:131
  9.5 99.2 %all-gather.16.cloned.1.call-start = ((), (), s32[]{:S(2)}) async-start(), calls=%async_computation.8 | async-start | bytes 4718592 | tf_op jit(solution)/shard_map/all_gather | solution.py:131
  10.2 128.2 %all-gather.10.cloned.1.call-start = ((), (), s32[]{:S(2)}) async-start(), calls=%async_computation.4 | async-start | bytes 2359296 | tf_op jit(solution)/shard_map/all_gather | solution.py:131
  28.4 161.4 %all-gather.14.cloned.1.call-start = ((), (), s32[]{:S(2)}) async-start(), calls=%async_computation.7 | async-start | bytes 4718592 | tf_op jit(solution)/shard_map/all_gather | solution.py:131
  30.5 40.2 %all-to-all-start = ((f32[8,512,128]{2,1,0:T(8,128)}), f32[8,512,128]{2,1,0:T(8,128)S(1)}, u32[]{:S(2)}, u32[]{:S(2)}) async-start(f32[8,512,128]{2,1,0:T(8,128)} %broadcast_in_dim.2), calls=%async_computation | async-start | bytes 4194304 | tf_op jit(solution)/shard_map/all_to_all | solution.py:136
  34.2 185.4 %all-gather.12.cloned.1.call-start = ((), (), s32[]{:S(2)}) async-start(), calls=%async_computation.6 | async-start | bytes 4718592 | tf_op jit(solution)/shard_map/all_gather | solution.py:131
  34.8 297.0 %reduce-scatter.2.cloned.1.call-start = ((), (), s32[]{:S(2)}) async-start(), calls=%async_computation.5 | async-start | bytes 2359296 | tf_op jit(solution)/shard_map/reduce_scatter | solution.py:152
  40.2 5.2 %copy-start = (f32[2048,512]{0,1:T(8,128)S(1)}, f32[2048,512]{0,1:T(8,128)}, u32[]{:S(2)}) copy-start(f32[2048,512]{0,1:T(8,128)} %copy.8) | copy-start | bytes 12582916
  70.6 1.3 copy-start.1
  331.7 6.5 %copy-start.4 = (f32[128]{0:T(128)S(1)}, f32[128]{0:T(128)}, u32[]{:S(2)}) copy-start(f32[128]{0:T(128)} %param.10) | copy-start | bytes 1540
  331.7 6.5 %copy-start.5 = (f32[128]{0:T(128)S(1)}, f32[128]{0:T(128)}, u32[]{:S(2)}) copy-start(f32[128]{0:T(128)} %param.11) | copy-start | bytes 1540
  331.7 20.5 %copy-start.3 = (f32[2,128,128]{2,1,0:T(8,128)S(1)}, f32[2,128,128]{2,1,0:T(8,128)}, u32[]{:S(2)}) copy-start(f32[2,128,128]{2,1,0:T(8,128)} %param.6) | copy-start | bytes 393220
  333.6 18.5 %all-to-all-start.2 = ((f32[4,2,128,128]{3,2,1,0:T(8,128)}), f32[4,2,128,128]{3,2,1,0:T(8,128)S(1)}, u32[]{:S(2)}, u32[]{:S(2)}) async-start(f32[4,2,128,128]{3,2,1,0:T(8,128)} %copy.9), calls=%async_computation.3 | async-start | bytes 1048576 | tf_op jit(solution)/shard_map/all_to_all | solution.py:171
Sparse Core Ops, SparseCore 0:
  9.6 54.9 all-gather.17
  66.5 42.2 all-gather.15
  110.6 27.7 all-gather.9
  140.2 36.5 all-gather.13
  178.5 36.5 all-gather.11
  249.2 41.0 reduce-scatter.1
